TPU v7x, 32 devices: a whole 2x2x4 slice. The times are simulated.
32 devices in a mesh: dp: 4 (over z), expert: 4 (over y, x), tensor: 2 (over core).
Axes of the slice: x: 2, y: 2, z: 4, core: 2. Of those that a mesh axis runs over, the one named last changes fastest.
Arguments:
- tokens: bfloat16 [512, 6144], P('dp'), may hold values from -6 to 6
- norm_gain: float32 [6144], replicated, may hold values from 0.1 to 1.9
- expert_ids: int32 [512, 2], P('dp'), may hold values from 0 to 3, all different within a row; in each aligned block of 128 rows (0 to 127, 128 to 255, ...) at most 72 rows name the same one
- gate_weights: float32 [512, 2], P('dp'), may hold values from 0.1 to 0.9
- w_gate: bfloat16 [4, 6144, 12288], P('expert', None, ('dp', 'tensor')), may hold values from -0.078125 to 0.078125
- w_up: bfloat16 [4, 6144, 12288], P('expert', None, ('dp', 'tensor')), may hold values from -0.078125 to 0.078125
- w_down: bfloat16 [4, 12288, 6144], P('expert', 'dp', 'tensor'), may hold values from -0.0546875 to 0.0546875
- label_rows: bfloat16 [512, 6144], P(('dp', 'expert'), 'tensor'), may hold values from -4 to 4, as said below
- seg_ids: int32 [4, 128], P('dp'), may hold values from 0 to 3, never falling along the last dimension, each value on 1 to 64 neighbouring positions
- pair_slot: int32 [4, 4], P('dp'), may hold values from 0 to 3, each once within a row
- ref_scores: float32 [4, 4], P('dp'), may hold values from -8 to 8
Outputs:
- layer_out: bfloat16 [512, 6144], P(('dp', 'expert'), 'tensor')
- margins: float32 [4, 2], P('dp')
Inputs may be any that keep to these rules, and one draw needn't show every extreme that they name: `expert_ids`: each row names two different experts. Among the 128 rows of one dp group no expert is named more than 72 times, and in some group some expert is named exactly 72 times. `seg_ids`: within each row sequence numbers never fall; every sequence has 1 to 64 tokens and one has exactly 64. `pair_slot`: each row holds every number of 0 to 3 once. `label_rows`: entries lie within 27 / sqrt(6144) in magnitude.
All inputs are finite; a program needn't handle non-finite values.
Results may differ from a plain program's by a relative error of at most 0.009.
Values may be sent and summed in bfloat16 or wider, within the bound.
A program may use at most 128 MiB of HBM per device.

v0:
```python
import jax
import jax.numpy as jnp
from jax import lax
from jax.sharding import PartitionSpec as P

SEQS = 4
PAIRS = 2
epsilon = 1e-05
dpo_beta = 0.5


def normed_rows(tokens, norm_gain):
    values = tokens.astype(jnp.float32)
    inverse_rms = lax.rsqrt(jnp.mean(values * values, axis=1, keepdims=True) + epsilon)
    return (values * inverse_rms * norm_gain[None, :]).astype(jnp.bfloat16)


def slot_tables(expert_ids, gate_weights, experts, capacity):
    tok_count = expert_ids.shape[0]
    flat_ids = expert_ids.reshape(-1)
    onehot = (flat_ids[:, None] == jnp.arange(experts, dtype=jnp.int32)[None, :]).astype(jnp.int32)
    earlier = jnp.cumsum(onehot, axis=0) - onehot
    position = jnp.sum(earlier * onehot, axis=1)
    slot_index = flat_ids * capacity + position
    slot_match = (
        slot_index[:, None] == jnp.arange(experts * capacity, dtype=jnp.int32)[None, :]
    ).astype(jnp.float32)
    slot_match = slot_match.reshape(tok_count, 2, experts * capacity)
    placement = jnp.sum(slot_match, axis=1)
    mixing = jnp.sum(slot_match * gate_weights[:, :, None], axis=1)
    return (placement, mixing)


def body(
    tokens,
    norm_gain,
    expert_ids,
    gate_weights,
    w_gate,
    w_up,
    w_down,
    label_rows,
    seg_ids,
    pair_slot,
    ref_scores,
):
    group_count = tokens.shape[0]
    experts = lax.axis_size("expert")
    expert_index = lax.axis_index("expert")
    capacity = max(2, 9 * group_count // (4 * experts))
    tensor_count = lax.axis_size("tensor")
    column_width = tokens.shape[1] // tensor_count
    tensor_index = lax.axis_index("tensor")
    own_count = group_count // experts
    normed = normed_rows(tokens, norm_gain)
    placement, mixing = slot_tables(expert_ids, gate_weights, experts, capacity)
    own_place = lax.dynamic_slice_in_dim(placement, expert_index * capacity, capacity, 1)
    own_mixing = lax.dynamic_slice_in_dim(mixing, expert_index * capacity, capacity, 1)
    arrived = jnp.dot(
        own_place.T.astype(jnp.bfloat16), normed, preferred_element_type=jnp.float32
    ).astype(jnp.bfloat16)
    gate_local = w_gate[0]
    up_local = w_up[0]
    down_local = w_down[0]
    own_columns = lax.dynamic_slice_in_dim(arrived, tensor_index * column_width, column_width, 1)
    group_rows = lax.all_gather(own_columns, "dp", axis=0, tiled=True)
    block_cols = lax.all_gather(group_rows, "tensor", axis=1, tiled=True)
    gate_sum = jnp.dot(block_cols, gate_local, preferred_element_type=jnp.float32)
    up_sum = jnp.dot(block_cols, up_local, preferred_element_type=jnp.float32)
    hidden = (jax.nn.silu(gate_sum) * up_sum).astype(jnp.bfloat16)
    hidden_block = lax.all_gather(hidden, "tensor", axis=1, tiled=True)
    own_rows = lax.psum_scatter(
        jnp.dot(hidden_block, down_local, preferred_element_type=jnp.float32).astype(jnp.bfloat16),
        "dp",
        scatter_dimension=0,
        tiled=True,
    )
    weighted = jnp.dot(own_mixing, own_rows.astype(jnp.float32), precision=lax.Precision.HIGHEST)
    expert_mix = lax.psum_scatter(
        weighted.astype(jnp.bfloat16), "expert", scatter_dimension=0, tiled=True
    ).astype(jnp.float32)
    token_rows = lax.dynamic_slice_in_dim(tokens, expert_index * own_count, own_count, 0)
    residual = lax.dynamic_slice_in_dim(
        token_rows, tensor_index * column_width, column_width, 1
    ).astype(jnp.float32)
    mixed = residual + expert_mix
    layer_out = mixed.astype(jnp.bfloat16)
    token_score = jnp.sum(mixed * label_rows.astype(jnp.float32), axis=1)
    sequence_ids = lax.dynamic_slice_in_dim(seg_ids[0], expert_index * own_count, own_count, 0)
    member = (sequence_ids[:, None] == jnp.arange(SEQS, dtype=jnp.int32)[None, :]).astype(
        jnp.float32
    )
    partial_value = jnp.sum(member * token_score[:, None], axis=0)
    totals = lax.psum(partial_value, ("expert", "tensor"))
    slots_here = pair_slot[0]
    polarity = (1 - 2 * (slots_here % 2)).astype(jnp.float32)
    pair_member = (
        (slots_here // 2)[:, None] == jnp.arange(PAIRS, dtype=jnp.int32)[None, :]
    ).astype(jnp.float32)
    margins = dpo_beta * jnp.sum(
        pair_member * (polarity * (totals - ref_scores[0]))[:, None], axis=0
    )
    return (layer_out, margins[None, :])


def solution(mesh):
    placed = (
        P("dp", None),
        P(),
        P("dp", None),
        P("dp", None),
        P("expert", None, ("dp", "tensor")),
        P("expert", None, ("dp", "tensor")),
        P("expert", "dp", "tensor"),
        P(("dp", "expert"), "tensor"),
        P("dp", None),
        P("dp", None),
        P("dp", None),
    )
    return jax.shard_map(
        body,
        mesh=mesh,
        in_specs=placed,
        out_specs=(P(("dp", "expert"), "tensor"), P("dp", None)),
        check_vma=False,
    )
```

profile of v0, /device:TPU:0, one launch (start us, length us, event | category | flops | bytes accessed | tf_op | source)
XLA Modules:
  0.0 209.0 jit_solution(1095833018729671077)
XLA Ops:
  7.2 0.8 copy.31
  8.0 0.1 eq.73
  8.2 0.1 eq.69
  8.3 1.2 reduce-window.6
  10.0 0.1 reduce_sum.66
  10.2 0.7 multiply_add_fusion
  10.9 1.8 fusion.9
  12.7 0.8 select_reduce_fusion
  13.4 2.1 %fusion.18 = bf16[72,6144]{1,0:T(8,128)(2,1)S(1)} fusion(bf16[128,6144]{1,0:T(8,128)(2,1)} %param.11, f32[6144]{0:T(1024)} %param.12, f32[128]{0:T(128)S(1)} %add_rsqrt_fusion, bf16[128,288]{0,1:T(8,128)(2,1)S(1)} %get-tuple-element.3, s32[]{:T(128)S(6)} %select_n.36), kind=kOutput, calls=%fused_computation.15 | convolution fusion | flops 116391936 | bytes 2501124 | tf_op jit(solution)/shard_map/dot_general | solution.py:59
  15.5 0.8 dynamic-slice_convert_fusion
  16.4 43.1 %all-gather.4.cloned.1.call-done = bf16[288,3072]{1,0:T(8,128)(2,1)} async-done(((bf16[72,3072]{1,0:T(8,128)(2,1)}), bf16[288,3072]{1,0:T(8,128)(2,1)}) %all-gather.4.cloned.1.call-update) | async-done | bytes 1769488 | tf_op jit(solution)/shard_map/all_gather | solution.py:66
  59.6 13.0 %all-gather.6.cloned.1.call-done = bf16[288,6144]{1,0:T(8,128)(2,1)} async-done(((bf16[288,3072]{1,0:T(8,128)(2,1)}), bf16[288,6144]{1,0:T(8,128)(2,1)}) %all-gather.6.cloned.1.call-update) | async-done | bytes 3538960 | tf_op jit(solution)/shard_map/all_gather | solution.py:67
  72.6 13.2 %fusion.4 = f32[288,1536]{1,0:T(8,128)S(1)} fusion(bf16[288,6144]{1,0:T(8,128)(2,1)} %all-gather.6.cloned.1.call-done, bf16[1,6144,1536]{2,1,0:T(8,128)(2,1)} %param.15), kind=kOutput, calls=%fused_computation.4 | convolution fusion | flops 5435817984 | bytes 24182784 | tf_op jit(solution)/shard_map/dot_general | solution.py:68
  85.8 11.0 %fusion.15 = bf16[288,1536]{1,0:T(8,128)(2,1)} fusion(bf16[288,6144]{1,0:T(8,128)(2,1)S(1)} %copy-done.4, bf16[1,6144,1536]{2,1,0:T(8,128)(2,1)} %param.16, f32[288,1536]{1,0:T(8,128)S(1)} %fusion.4), kind=kOutput, calls=%fused_computation.14 | convolution fusion | flops 5438472192 | bytes 25067520 | tf_op jit(solution)/shard_map/dot_general | solution.py:69
  96.9 11.4 %all-gather.8.cloned.1.call-done = bf16[288,3072]{1,0:T(8,128)(2,1)} async-done(((bf16[288,1536]{1,0:T(8,128)(2,1)}), bf16[288,3072]{1,0:T(8,128)(2,1)}) %all-gather.8.cloned.1.call-update) | async-done | bytes 1769488 | tf_op jit(solution)/shard_map/all_gather | solution.py:71
  108.3 11.1 %fusion.6 = bf16[288,3072]{1,0:T(8,128)(2,1)} fusion(bf16[288,3072]{1,0:T(8,128)(2,1)} %all-gather.8.cloned.1.call-done, bf16[1,3072,3072]{2,1,0:T(8,128)(2,1)} %param.17), kind=kOutput, calls=%fused_computation.6 | convolution fusion | flops 5436702720 | bytes 22413312 | tf_op jit(solution)/shard_map/dot_general | solution.py:73
  119.4 39.8 %reduce-scatter.3.cloned.1.call-done = bf16[72,3072]{1,0:T(8,128)(2,1)} async-done(((bf16[288,3072]{1,0:T(8,128)(2,1)}), bf16[72,3072]{1,0:T(8,128)(2,1)}) %reduce-scatter.3.cloned.1.call-update) | async-done | bytes 442384 | tf_op jit(solution)/shard_map/reduce_scatter | solution.py:72
  159.2 2.7 %convolution_convert_fusion = bf16[128,3072]{1,0:T(8,128)(2,1)} fusion(bf16[72,3072]{1,0:T(8,128)(2,1)} %reduce-scatter.3.cloned.1.call-done, f32[128,288]{0,1:T(8,128)S(1)} %get-tuple-element.2, s32[]{:T(128)S(6)} %select_n.36), kind=kOutput, calls=%fused_computation.9 | convolution fusion | flops 340131840 | bytes 1265668 | tf_op jit(solution)/shard_map/dot_general | solution.py:78
  162.0 25.2 %reduce-scatter.5.cloned.1.call-done = bf16[32,3072]{1,0:T(8,128)(2,1)} async-done(((bf16[128,3072]{1,0:T(8,128)(2,1)}), bf16[32,3072]{1,0:T(8,128)(2,1)}) %reduce-scatter.5.cloned.1.call-update) | async-done | bytes 196624 | tf_op jit(solution)/shard_map/reduce_scatter | solution.py:79
  187.2 2.0 multiply_reduce_fusion
  189.2 0.1 select_reduce_fusion.1
  189.4 12.5 %psum.7 = f32[4]{0:T(128)S(1)} all-reduce(f32[4]{0:T(128)S(1)} %select_reduce_fusion.1), channel_id=1, replica_groups=mesh['dp'=4,'expert'=4,'tensor'=2] {'expert','tensor'}, use_global_device_ids=true, to_apply=%region_10.11 | all-reduce | flops 4 | bytes 32 | tf_op jit(solution)/shard_map/psum | solution.py:94
  201.8 0.1 fusion.27
  201.9 0.5 multiply_bitcast_fusion
  (33 shorter events, 0.9 us)
Async XLA Ops:
  7.2 154.8 %copy-start = (s32[1,128]{1,0:T(1,128)S(1)}, s32[1,128]{1,0:T(1,128)}, u32[]{:S(2)}) copy-start(s32[1,128]{1,0:T(1,128)} %param.19) | copy-start | bytes 1540
  7.2 52.3 %all-gather.4.cloned.1.call-start = ((), (), s32[]{:S(2)}) async-start(), calls=%async_computation.2 | async-start | bytes 2211840 | tf_op jit(solution)/shard_map/all_gather | solution.py:66
  16.4 56.2 %all-gather.6.cloned.1.call-start = ((), (), s32[]{:S(2)}) async-start(), calls=%async_computation.3 | async-start | bytes 5308416 | tf_op jit(solution)/shard_map/all_gather | solution.py:67
  59.5 48.7 %all-gather.8.cloned.1.call-start = ((), (), s32[]{:S(2)}) async-start(), calls=%async_computation.4 | async-start | bytes 2654208 | tf_op jit(solution)/shard_map/all_gather | solution.py:71
  72.6 13.2 %copy-start.4 = (bf16[288,6144]{1,0:T(8,128)(2,1)S(1)}, bf16[288,6144]{1,0:T(8,128)(2,1)}, u32[]{:S(2)}) copy-start(bf16[288,6144]{1,0:T(8,128)(2,1)} %all-gather.6.cloned.1.call-done) | copy-start | bytes 10616836
  96.8 62.4 %reduce-scatter.3.cloned.1.call-start = ((), (), s32[]{:S(2)}) async-start(), calls=%async_computation.5 | async-start | bytes 2211840 | tf_op jit(solution)/shard_map/reduce_scatter | solution.py:72
  119.4 67.9 %copy-start.1 = (bf16[32,3072]{1,0:T(8,128)(2,1)S(1)}, bf16[32,3072]{1,0:T(8,128)(2,1)}, u32[]{:S(2)}) copy-start(bf16[32,3072]{1,0:T(8,128)(2,1)} %param.18) | copy-start | bytes 589828
  119.4 70.0 %copy-start.3 = (s32[1,4]{1,0:T(1,128)S(1)}, s32[1,4]{1,0:T(1,128)}, u32[]{:S(2)}) copy-start(s32[1,4]{1,0:T(1,128)} %param.20) | copy-start | bytes 52
  119.4 82.5 %copy-start.2 = (f32[1,4]{1,0:T(1,128)S(1)}, f32[1,4]{1,0:T(1,128)}, u32[]{:S(2)}) copy-start(f32[1,4]{1,0:T(1,128)} %param.21) | copy-start | bytes 52
  119.4 67.8 %reduce-scatter.5.cloned.1.call-start = ((), (), s32[]{:S(2)}) async-start(), calls=%async_computation.6 | async-start | bytes 983040 | tf_op jit(solution)/shard_map/reduce_scatter | solution.py:79
Sparse Core Ops, SparseCore 0:
  16.5 42.9 all-gather.3
  61.1 11.5 all-gather.5
  97.0 11.2 all-gather.7
  119.5 39.6 reduce-scatter.2
  162.1 25.1 reduce-scatter.4
where the time goes:
time: 209 us
  waiting for transfers between devices  133 us (64%)
  matrix products  40.1 us (19%)
  between operations  13.9 us (7%)
  blocking collectives  12.5 us (6%)
  other arithmetic  7.38 us (4%)
  local copies, waits for them, and re-layouts  2.45 us (1%)
    all_gather x1, waiting for transfers between devices, body(): group_rows = lax.all_gather(own_columns, 'dp', axis=0, tiled=True)  43.1 us
    reduce_scatter x1, waiting for transfers between devices, body(): lax.psum_scatter(jnp.dot(hidden_block, down_local, preferred_element_type...  39.8 us
    reduce_scatter x1, waiting for transfers between devices, body(): lax.psum_scatter(weighted.astype(jnp.bfloat16), 'expert', scatter_dimensi...  25.2 us
    dot_general x1, matrix products, body(): jnp.dot(block_cols, gate_local, preferred_element_type=jnp.float32)  13.2 us
    all_gather x1, waiting for transfers between devices, body(): block_cols = lax.all_gather(group_rows, 'tensor', axis=1, tiled=True)  13 us
    psum x1, blocking collectives, body(): totals = lax.psum(partial_value, ('expert', 'tensor'))  12.5 us
    all_gather x1, waiting for transfers between devices, body(): hidden_block = lax.all_gather(hidden, 'tensor', axis=1, tiled=True)  11.4 us
    dot_general x1, matrix products, body(): jnp.dot(hidden_block, down_local, preferred_element_type=jnp.float32)  11.1 us
  transfers between devices with their start and end apart: 5, of which 5 were waited for; matrix products, arithmetic and copies ran while one was open for 0% of the time, Pallas kernels for 0%

commit v1 on v0

--- a/solution.py
+++ b/solution.py
@@ -7,6 +7,17 @@
 PAIRS = 2
 epsilon = 1e-05
 dpo_beta = 0.5
+
+
+def around_the_ring(x, axis, dim):
+    size = lax.axis_size(axis)
+    hops = [(i, (i + 1) % size) for i in range(size)]
+    terms = [x]
+    for hop in range(1, size):
+        terms = [lax.ppermute(terms[0], axis, hops), *terms]
+    out = jnp.concatenate(terms, axis=dim)
+    turn = (lax.axis_index(axis) + 1) * terms[-1].shape[dim]
+    return jnp.roll(out, turn, axis=dim)
 
 
 def normed_rows(tokens, norm_gain):
@@ -63,7 +74,7 @@
     up_local = w_up[0]
     down_local = w_down[0]
     own_columns = lax.dynamic_slice_in_dim(arrived, tensor_index * column_width, column_width, 1)
-    group_rows = lax.all_gather(own_columns, "dp", axis=0, tiled=True)
+    group_rows = around_the_ring(own_columns, "dp", 0)
     block_cols = lax.all_gather(group_rows, "tensor", axis=1, tiled=True)
     gate_sum = jnp.dot(block_cols, gate_local, preferred_element_type=jnp.float32)
     up_sum = jnp.dot(block_cols, up_local, preferred_element_type=jnp.float32)

time: 209 us -> 206 us (0.986)
  waiting for transfers between devices: 133 us -> 125 us
  starting transfers between devices: 0.2 us -> 3.27 us
    all_gather x1 -> x0, waiting for transfers between devices: 43.1 us -> none  [body(): group_rows = lax.all_gather(own_columns, 'dp', axis=0, tiled=True)]
    ppermute x0 -> x3, waiting for transfers between devices: none -> 37.6 us  [around_the_ring(): terms = [lax.ppermute(terms[0], axis, hops), *terms]]
    ppermute x0 -> x3, starting transfers between devices: none -> 3.11 us  [around_the_ring(): terms = [lax.ppermute(terms[0], axis, hops), *terms]]
    all_gather x1, waiting for transfers between devices: 13 us -> 10.6 us  [body(): block_cols = lax.all_gather(group_rows, 'tensor', axis=1, tiled=True)]
  transfers between devices with their start and end apart: 5 -> 7, of which waited for: 5 -> 7; matrix products, arithmetic and copies ran while one was open for 0% -> 0% of each run, Pallas kernels for 0% -> 0%
where the time goes in v1:
time: 206 us; the launch traced here: 205 us
  waiting for transfers between devices  125 us (61%)
  matrix products  40.1 us (19%)
  between operations  13.9 us (7%)
  blocking collectives  12.5 us (6%)
  other arithmetic  7.38 us (4%)
  local copies, waits for them, and re-layouts  3.61 us (2%)
  starting transfers between devices  3.27 us (2%)
    reduce_scatter x1, waiting for transfers between devices, body(): lax.psum_scatter(jnp.dot(hidden_block, down_local, preferred_element_type...  39.8 us
    ppermute x3, waiting for transfers between devices, around_the_ring(): terms = [lax.ppermute(terms[0], axis, hops), *terms]  37.6 us
    reduce_scatter x1, waiting for transfers between devices, body(): lax.psum_scatter(weighted.astype(jnp.bfloat16), 'expert', scatter_dimensi...  25.2 us
    dot_general x1, matrix products, body(): jnp.dot(block_cols, gate_local, preferred_element_type=jnp.float32)  13.2 us
    psum x1, blocking collectives, body(): totals = lax.psum(partial_value, ('expert', 'tensor'))  12.5 us
    all_gather x1, waiting for transfers between devices, body(): hidden_block = lax.all_gather(hidden, 'tensor', axis=1, tiled=True)  11.3 us
    dot_general x1, matrix products, body(): jnp.dot(hidden_block, down_local, preferred_element_type=jnp.float32)  11.1 us
    dot_general x1, matrix products, body(): up_sum = jnp.dot(block_cols, up_local, preferred_element_type=jnp.float32)  11 us
  transfers between devices with their start and end apart: 7, of which 7 were waited for; matrix products, arithmetic and copies ran while one was open for 0% of the time, Pallas kernels for 0%

profile of v1, /device:TPU:0, one launch (start us, length us, event | category | flops | bytes accessed | tf_op | source)
XLA Modules:
  0.0 205.3 jit_solution(9844908278757200093)
XLA Ops:
  7.2 0.8 copy.31
  8.2 0.1 eq.72
  8.3 1.2 reduce-window.6
  10.0 0.1 reduce_sum.66
  10.2 0.7 multiply_add_fusion
  10.9 1.8 fusion.9
  12.7 0.8 select_reduce_fusion
  13.4 2.1 %fusion.18 = bf16[72,6144]{1,0:T(8,128)(2,1)S(1)} fusion(bf16[128,6144]{1,0:T(8,128)(2,1)} %param.11, f32[6144]{0:T(1024)} %param.12, f32[128]{0:T(128)S(1)} %add_rsqrt_fusion, bf16[128,288]{0,1:T(8,128)(2,1)S(1)} %get-tuple-element.3, s32[]{:T(128)S(6)} %select_n.48), kind=kOutput, calls=%fused_computation.15 | convolution fusion | flops 116391936 | bytes 2501124 | tf_op jit(solution)/shard_map/dot_general | solution.py:70
  15.6 3.1 %collective-permute-start = (bf16[72,3072]{1,0:T(8,128)(2,1)S(1)}, bf16[72,3072]{1,0:T(8,128)(2,1)S(1)}, u32[]{:S(2)}, u32[]{:S(2)}) collective-permute-start(bf16[72,3072]{1,0:T(8,128)(2,1)S(1)} %dynamic-slice_convert_fusion), channel_id=1, source_target_pairs={{0,8},{8,16},{16,24},{24,0},{1,9},{9,17},{17,25},{25,1},{2,10},{10... | collective-permute-start | bytes 1327112 | tf_op jit(solution)/shard_map/ppermute | solution.py:17
  18.7 12.2 %collective-permute-done = bf16[72,3072]{1,0:T(8,128)(2,1)S(1)} collective-permute-done((bf16[72,3072]{1,0:T(8,128)(2,1)S(1)}, bf16[72,3072]{1,0:T(8,128)(2,1)S(1)}, u32[]{:S(2)}, u32[]{:S(2)}) %collective-permute-start) | collective-permute-done | bytes 442400 | tf_op jit(solution)/shard_map/ppermute | solution.py:17
  30.9 13.1 %collective-permute-done.1 = bf16[72,3072]{1,0:T(8,128)(2,1)S(1)} collective-permute-done((bf16[72,3072]{1,0:T(8,128)(2,1)S(1)}, bf16[72,3072]{1,0:T(8,128)(2,1)S(1)}, u32[]{:S(2)}, u32[]{:S(2)}) %collective-permute-start.1) | collective-permute-done | bytes 442400 | tf_op jit(solution)/shard_map/ppermute | solution.py:17
  44.0 12.3 %collective-permute-done.2 = bf16[72,3072]{1,0:T(8,128)(2,1)S(1)} collective-permute-done((bf16[72,3072]{1,0:T(8,128)(2,1)S(1)}, bf16[72,3072]{1,0:T(8,128)(2,1)S(1)}, u32[]{:S(2)}, u32[]{:S(2)}) %collective-permute-start.2) | collective-permute-done | bytes 442400 | tf_op jit(solution)/shard_map/ppermute | solution.py:17
  56.6 1.7 constant_dynamic-slice_fusion
  58.4 10.6 %all-gather.3.cloned.1.call-done = bf16[288,6144]{1,0:T(8,128)(2,1)} async-done(((bf16[288,3072]{1,0:T(8,128)(2,1)}), bf16[288,6144]{1,0:T(8,128)(2,1)}) %all-gather.3.cloned.1.call-update) | async-done | bytes 3538960 | tf_op jit(solution)/shard_map/all_gather | solution.py:78
  68.9 13.2 %fusion.4 = f32[288,1536]{1,0:T(8,128)S(1)} fusion(bf16[288,6144]{1,0:T(8,128)(2,1)} %all-gather.3.cloned.1.call-done, bf16[1,6144,1536]{2,1,0:T(8,128)(2,1)} %param.15), kind=kOutput, calls=%fused_computation.4 | convolution fusion | flops 5435817984 | bytes 24182784 | tf_op jit(solution)/shard_map/dot_general | solution.py:79
  82.1 11.0 %fusion.15 = bf16[288,1536]{1,0:T(8,128)(2,1)} fusion(bf16[288,6144]{1,0:T(8,128)(2,1)S(1)} %copy-done.4, bf16[1,6144,1536]{2,1,0:T(8,128)(2,1)} %param.16, f32[288,1536]{1,0:T(8,128)S(1)} %fusion.4), kind=kOutput, calls=%fused_computation.14 | convolution fusion | flops 5438472192 | bytes 25067520 | tf_op jit(solution)/shard_map/dot_general | solution.py:80
  93.2 11.3 %all-gather.5.cloned.1.call-done = bf16[288,3072]{1,0:T(8,128)(2,1)} async-done(((bf16[288,1536]{1,0:T(8,128)(2,1)}), bf16[288,3072]{1,0:T(8,128)(2,1)}) %all-gather.5.cloned.1.call-update) | async-done | bytes 1769488 | tf_op jit(solution)/shard_map/all_gather | solution.py:82
  104.6 11.1 %fusion.6 = bf16[288,3072]{1,0:T(8,128)(2,1)} fusion(bf16[288,3072]{1,0:T(8,128)(2,1)} %all-gather.5.cloned.1.call-done, bf16[1,3072,3072]{2,1,0:T(8,128)(2,1)} %param.17), kind=kOutput, calls=%fused_computation.6 | convolution fusion | flops 5436702720 | bytes 22413312 | tf_op jit(solution)/shard_map/dot_general | solution.py:84
  115.7 39.8 %reduce-scatter.3.cloned.1.call-done = bf16[72,3072]{1,0:T(8,128)(2,1)} async-done(((bf16[288,3072]{1,0:T(8,128)(2,1)}), bf16[72,3072]{1,0:T(8,128)(2,1)}) %reduce-scatter.3.cloned.1.call-update) | async-done | bytes 442384 | tf_op jit(solution)/shard_map/reduce_scatter | solution.py:83
  155.5 2.7 %convolution_convert_fusion = bf16[128,3072]{1,0:T(8,128)(2,1)} fusion(bf16[72,3072]{1,0:T(8,128)(2,1)} %reduce-scatter.3.cloned.1.call-done, f32[128,288]{0,1:T(8,128)S(1)} %get-tuple-element.2, s32[]{:T(128)S(6)} %select_n.48), kind=kOutput, calls=%fused_computation.9 | convolution fusion | flops 340131840 | bytes 1265668 | tf_op jit(solution)/shard_map/dot_general | solution.py:89
  158.3 25.2 %reduce-scatter.5.cloned.1.call-done = bf16[32,3072]{1,0:T(8,128)(2,1)} async-done(((bf16[128,3072]{1,0:T(8,128)(2,1)}), bf16[32,3072]{1,0:T(8,128)(2,1)}) %reduce-scatter.5.cloned.1.call-update) | async-done | bytes 196624 | tf_op jit(solution)/shard_map/reduce_scatter | solution.py:90
  183.5 2.0 multiply_reduce_fusion
  185.7 12.5 %psum.7 = f32[4]{0:T(128)S(1)} all-reduce(f32[4]{0:T(128)S(1)} %select_reduce_fusion.1), channel_id=1, replica_groups=mesh['dp'=4,'expert'=4,'tensor'=2] {'expert','tensor'}, use_global_device_ids=true, to_apply=%region_10.11 | all-reduce | flops 4 | bytes 32 | tf_op jit(solution)/shard_map/psum | solution.py:105
  198.3 0.5 multiply_bitcast_fusion
  (45 shorter events, 1.5 us)
Async XLA Ops:
  7.2 151.1 %copy-start = (s32[1,128]{1,0:T(1,128)S(1)}, s32[1,128]{1,0:T(1,128)}, u32[]{:S(2)}) copy-start(s32[1,128]{1,0:T(1,128)} %param.19) | copy-start | bytes 1540
  7.2 61.8 %all-gather.3.cloned.1.call-start = ((), (), s32[]{:S(2)}) async-start(), calls=%async_computation.2 | async-start | bytes 5308416 | tf_op jit(solution)/shard_map/all_gather | solution.py:78
  15.6 15.3 %collective-permute-start = (bf16[72,3072]{1,0:T(8,128)(2,1)S(1)}, bf16[72,3072]{1,0:T(8,128)(2,1)S(1)}, u32[]{:S(2)}, u32[]{:S(2)}) collective-permute-start(bf16[72,3072]{1,0:T(8,128)(2,1)S(1)} %dynamic-slice_convert_fusion), channel_id=1, source_target_pairs={{0,8},{8,16},{16,24},{24,0},{1,9},{9,17},{17,25},{25,1},{2,10},{10... | collective-permute-start | bytes 1327112 | tf_op jit(solution)/shard_map/ppermute | solution.py:17
  30.9 13.1 %collective-permute-start.1 = (bf16[72,3072]{1,0:T(8,128)(2,1)S(1)}, bf16[72,3072]{1,0:T(8,128)(2,1)S(1)}, u32[]{:S(2)}, u32[]{:S(2)}) collective-permute-start(bf16[72,3072]{1,0:T(8,128)(2,1)S(1)} %collective-permute-done), channel_id=1, source_target_pairs={{0,8},{8,16},{16,24},{24,0},{1,9},{9,17},{17,25},{25,1},{2,10},{10... | collective-permute-start | bytes 1327112 | tf_op jit(solution)/shard_map/ppermute | solution.py:17
  44.0 12.3 %collective-permute-start.2 = (bf16[72,3072]{1,0:T(8,128)(2,1)S(1)}, bf16[72,3072]{1,0:T(8,128)(2,1)S(1)}, u32[]{:S(2)}, u32[]{:S(2)}) collective-permute-start(bf16[72,3072]{1,0:T(8,128)(2,1)S(1)} %collective-permute-done.1), channel_id=1, source_target_pairs={{0,8},{8,16},{16,24},{24,0},{1,9},{9,17},{17,25},{25,1},{2,10},{10... | collective-permute-start | bytes 1327112 | tf_op jit(solution)/shard_map/ppermute | solution.py:17
  58.3 46.3 %all-gather.5.cloned.1.call-start = ((), (), s32[]{:S(2)}) async-start(), calls=%async_computation.3 | async-start | bytes 2654208 | tf_op jit(solution)/shard_map/all_gather | solution.py:82
  68.9 13.2 %copy-start.4 = (bf16[288,6144]{1,0:T(8,128)(2,1)S(1)}, bf16[288,6144]{1,0:T(8,128)(2,1)}, u32[]{:S(2)}) copy-start(bf16[288,6144]{1,0:T(8,128)(2,1)} %all-gather.3.cloned.1.call-done) | copy-start | bytes 10616836
  93.2 62.3 %reduce-scatter.3.cloned.1.call-start = ((), (), s32[]{:S(2)}) async-start(), calls=%async_computation.4 | async-start | bytes 2211840 | tf_op jit(solution)/shard_map/reduce_scatter | solution.py:83
  115.7 67.9 %copy-start.1 = (bf16[32,3072]{1,0:T(8,128)(2,1)S(1)}, bf16[32,3072]{1,0:T(8,128)(2,1)}, u32[]{:S(2)}) copy-start(bf16[32,3072]{1,0:T(8,128)(2,1)} %param.18) | copy-start | bytes 589828
  115.7 70.0 %copy-start.3 = (s32[1,4]{1,0:T(1,128)S(1)}, s32[1,4]{1,0:T(1,128)}, u32[]{:S(2)}) copy-start(s32[1,4]{1,0:T(1,128)} %param.20) | copy-start | bytes 52
  115.7 82.5 %copy-start.2 = (f32[1,4]{1,0:T(1,128)S(1)}, f32[1,4]{1,0:T(1,128)}, u32[]{:S(2)}) copy-start(f32[1,4]{1,0:T(1,128)} %param.21) | copy-start | bytes 52
  115.7 67.8 %reduce-scatter.5.cloned.1.call-start = ((), (), s32[]{:S(2)}) async-start(), calls=%async_computation.5 | async-start | bytes 983040 | tf_op jit(solution)/shard_map/reduce_scatter | solution.py:90
Sparse Core Ops, SparseCore 0:
  58.4 10.4 all-gather.2
  93.3 11.2 all-gather.4
  115.8 39.6 reduce-scatter.2
  158.4 25.1 reduce-scatter.4
